TPU v7x, 32 devices: a whole 2x2x4 slice. The times are simulated.
32 devices in a mesh: rep: 2 (over y), sample: 4 (over z), head: 4 (over x, core).
Axes of the slice: x: 2, y: 2, z: 4, core: 2. Of those that a mesh axis runs over, the one named last changes fastest.
Arguments:
- x_pre: bfloat16 [8, 128, 8192], P(('rep', 'sample'), None, 'head'), parts along dimension 0, may hold values from -120 to 120
- z_pre: bfloat16 [8, 128, 8192], P(('rep', 'sample'), None, 'head'), parts along dimension 0, may hold values from -6 to 6
- b_pre: bfloat16 [8, 128, 512], P(('rep', 'sample')), parts along dimension 0, may hold values from -1.796875 to 1.796875
- c_pre: bfloat16 [8, 128, 512], P(('rep', 'sample')), parts along dimension 0, may hold values from -0.5390625 to 0.5390625
- dt_pre: float32 [8, 128, 128], P(('rep', 'sample'), None, 'head'), parts along dimension 0, may hold values from -1.5 to 7.5
- lengths: int32 [8], P(('rep', 'sample')), parts along dimension 0, may hold values from 64 to 128, as said below
- init_state: float32 [8, 128, 8192], P(('rep', 'sample'), None, 'head'), parts along dimension 0, may hold values from -6 to 6
- a_rates: float32 [128], P('head'), may hold values from 0.005 to 0.3
- dt_bias: float32 [128], P('head'), may hold values from -2 to -1
- skip_scale: float32 [128], P('head'), may hold values from 0.5 to 2
- norm_gain: float32 [8192], P('head'), may hold values from 0.5 to 1.5
- x_dec: bfloat16 [8, 4, 8192], P(('rep', 'sample'), None, 'head'), parts along dimension 0, may hold values from -120 to 120
- z_dec: bfloat16 [8, 4, 8192], P(('rep', 'sample'), None, 'head'), parts along dimension 0, may hold values from -6 to 6
- b_dec: bfloat16 [8, 4, 512], P(('rep', 'sample')), parts along dimension 0, may hold values from -6 to 6
- c_dec: bfloat16 [8, 4, 512], P(('rep', 'sample')), parts along dimension 0, may hold values from -0.5390625 to 0.5390625
- dt_dec: float32 [8, 4, 128], P(('rep', 'sample'), None, 'head'), parts along dimension 0, may hold values from -3 to 3
Outputs:
- out_pre: bfloat16 [8, 128, 8192], P(('rep', 'sample'), None, 'head'), parts along dimension 0
- final_state: bfloat16 [8, 128, 8192], P(('rep', 'sample'), None, 'head'), parts along dimension 0
- out_dec: bfloat16 [8, 4, 8192], P(('rep', 'sample'), None, 'head'), parts along dimension 0
There are 2 independent parts, one for each index of `rep`. A program takes and returns all parts, laid end to end along the dimension named above; an argument that names none is the same for every part. Nothing has to cross between parts.
Inputs may be any that keep to these rules, and one draw needn't show every extreme that they name: Each prompt's valid tokens are the first lengths[p] of its 128 positions; some prompt uses all 128.
All inputs are finite; a program needn't handle non-finite values.
Results may differ from a plain program's by a relative error of at most 0.006.
Values may be sent and summed in bfloat16 or wider, within the bound.
No kernel may reach another device: no remote copies, remote signals or barrier semaphores. Data moves between devices by JAX's collectives and lax.ppermute only.
A program may use at most 64 MiB of HBM per device.

v0:
```python
import jax
import jax.numpy as jnp
from jax import lax
from jax.sharding import PartitionSpec as P

H = 128
P_SIZE = 64
G = 4
BLOCK = 128
epsilon = 1e-05
highest = lax.Precision.HIGHEST


def group_owners(first_head, head_count):
    head_ids = first_head + jnp.arange(head_count, dtype=jnp.int32)
    return head_ids // (H // G)


def group_pick(owners):
    return (owners[:, None] == jnp.arange(G, dtype=jnp.int32)[None, :]).astype(jnp.float32)


def scan_prompt(inputs, b_rows, c_rows, step_delta, rates, skip_gain, start_state, owners):
    length = inputs.shape[0]
    head_count = step_delta.shape[1]
    head_width = inputs.shape[1] // head_count
    states = b_rows.shape[1] // G
    blocks = length // BLOCK
    b_groups = b_rows.reshape(blocks, BLOCK, G, states)
    c_groups = c_rows.reshape(blocks, BLOCK, G, states)
    group_scores = jnp.einsum(
        "cign,cjgn->cijg", c_groups, b_groups, preferred_element_type=jnp.float32
    )
    head_scores = jnp.take(group_scores, owners, axis=3)
    b_head = jnp.take(b_groups, owners, axis=2).astype(jnp.float32)
    c_head = jnp.take(c_groups, owners, axis=2).astype(jnp.float32)
    values = inputs.astype(jnp.float32).reshape(blocks, BLOCK, head_count, head_width)
    block_delta = step_delta.reshape(blocks, BLOCK, head_count)
    decays = jnp.cumsum(-block_delta * rates, axis=1)
    causal_mask = (jnp.arange(BLOCK)[:, None] >= jnp.arange(BLOCK)[None, :])[None, :, :, None]
    spread = decays[:, :, None, :] - decays[:, None, :, :]
    weights = jnp.where(causal_mask, jnp.exp(jnp.where(causal_mask, spread, 0.0)), 0.0)
    scores = head_scores * weights * block_delta[:, None, :, :]
    inner_part = jnp.einsum("cijh,cjhp->cihp", scores, values, precision=highest)
    tail_decay = jnp.exp(decays[:, -1:, :] - decays) * block_delta
    block_states = jnp.einsum(
        "cjhn,cjhp->cnhp", b_head * tail_decay[..., None], values, precision=highest
    )
    block_totals = jnp.exp(decays[:, -1, :])

    def carry_step(carried, pieces):
        factor, fresh_term = pieces
        return (factor[None, :, None] * carried + fresh_term, carried)

    final_carry, starts = lax.scan(
        carry_step,
        start_state.reshape(states, head_count, head_width),
        (block_totals, block_states),
    )
    outer_part = (
        jnp.einsum("cihn,cnhp->cihp", c_head, starts, precision=highest)
        * jnp.exp(decays)[..., None]
    )
    result = inner_part + outer_part + skip_gain[None, None, :, None] * values
    return (
        result.reshape(length, head_count * head_width),
        final_carry.reshape(states, head_count * head_width),
    )


def gate_values(result, gate_rows):
    gate_rows = gate_rows.astype(jnp.float32)
    return result * gate_rows * jax.nn.sigmoid(gate_rows)


def select_heads(c_rows, owners):
    shape_front = c_rows.shape[:2]
    states = c_rows.shape[2] // G
    grouped = c_rows.reshape(shape_front[0], shape_front[1], G, states)
    return jnp.take(grouped, owners, axis=2)


def body(
    x_pre,
    z_pre,
    b_pre,
    c_pre,
    dt_pre,
    lengths,
    init_state,
    a_rates,
    dt_bias,
    skip_scale,
    norm_gain,
    x_dec,
    z_dec,
    b_dec,
    c_dec,
    dt_dec,
):
    heads_here = a_rates.shape[0]
    head_width = x_pre.shape[2] // heads_here
    first_head = lax.axis_index("head") * heads_here
    owners = group_owners(first_head, heads_here)
    picker = group_pick(owners)
    length = x_pre.shape[1]
    positions = jnp.arange(length, dtype=jnp.int32)
    valid_mask = (positions[None, :] < lengths[:, None]).astype(jnp.float32)
    step_delta = jax.nn.softplus(dt_pre + dt_bias) * valid_mask[:, :, None]

    def one_prompt(pieces):
        inputs, b_rows, c_rows, prompt_delta, start_state = pieces
        return scan_prompt(
            inputs, b_rows, c_rows, prompt_delta, a_rates, skip_scale, start_state, owners
        )

    result, final_carry = lax.map(one_prompt, (x_pre, b_pre, c_pre, step_delta, init_state))
    final_state = final_carry.astype(jnp.bfloat16)
    gated_rows = gate_values(result, z_pre)
    pre_totals = lax.psum(jnp.sum(gated_rows * gated_rows, axis=-1), "head")
    norm_scale = lax.rsqrt(pre_totals[:, :, None] / (H * P_SIZE) + epsilon)
    out_pre = (gated_rows * norm_scale * norm_gain * valid_mask[:, :, None]).astype(jnp.bfloat16)
    slots_here = x_dec.shape[0]
    prompt_count = x_dec.shape[1]
    prompts_here = final_state.shape[0]
    states = final_state.shape[1]
    cached = final_state.reshape(prompts_here, states, heads_here, head_width)
    queries = lax.all_to_all(c_dec, "sample", split_axis=1, concat_axis=0, tiled=True)
    c_head = select_heads(queries, owners)
    answers = jnp.einsum("sphn,pnhq->sphq", c_head, cached, preferred_element_type=jnp.float32)
    answers = answers.reshape(answers.shape[0], prompts_here, heads_here * head_width)
    state_reads = lax.all_to_all(
        answers.astype(jnp.bfloat16), "sample", split_axis=0, concat_axis=1, tiled=True
    ).astype(answers.dtype)
    state_reads = state_reads.reshape(slots_here, prompt_count, heads_here, head_width)
    c_groups = c_dec.astype(jnp.float32).reshape(slots_here, prompt_count, G, states)
    b_groups = b_dec.astype(jnp.float32).reshape(slots_here, prompt_count, G, states)
    cb_dot = jnp.einsum("spgn,spgn->spg", c_groups, b_groups, precision=highest)
    cb_dot = jnp.einsum("spg,hg->sph", cb_dot, picker, precision=highest)
    step_sizes = jax.nn.softplus(dt_dec + dt_bias)
    decay_rate = jnp.exp(-step_sizes * a_rates)
    values = x_dec.astype(jnp.float32).reshape(slots_here, prompt_count, heads_here, head_width)
    fresh_term = (
        decay_rate[..., None] * state_reads + (step_sizes * cb_dot + skip_scale)[..., None] * values
    )
    gated_dec = gate_values(
        fresh_term.reshape(slots_here, prompt_count, heads_here * head_width), z_dec
    )
    dec_totals = lax.psum(jnp.sum(gated_dec * gated_dec, axis=-1), "head")
    dec_scale = lax.rsqrt(dec_totals[:, :, None] / (H * P_SIZE) + epsilon)
    out_dec = (gated_dec * dec_scale * norm_gain).astype(jnp.bfloat16)
    return (out_pre, final_state, out_dec)


def solution(mesh):
    in_specs = (
        P(("rep", "sample"), None, "head"),
        P(("rep", "sample"), None, "head"),
        P(("rep", "sample"), None, None),
        P(("rep", "sample"), None, None),
        P(("rep", "sample"), None, "head"),
        P(("rep", "sample")),
        P(("rep", "sample"), None, "head"),
        P("head"),
        P("head"),
        P("head"),
        P("head"),
        P(("rep", "sample"), None, "head"),
        P(("rep", "sample"), None, "head"),
        P(("rep", "sample"), None, None),
        P(("rep", "sample"), None, None),
        P(("rep", "sample"), None, "head"),
    )
    out_specs = (
        P(("rep", "sample"), None, "head"),
        P(("rep", "sample"), None, "head"),
        P(("rep", "sample"), None, "head"),
    )
    return jax.shard_map(body, mesh=mesh, in_specs=in_specs, out_specs=out_specs, check_vma=False)
```

profile of v0, /device:TPU:0, one launch (start us, length us, event | category | flops | bytes accessed | tf_op | source)
XLA Modules:
  0.0 61.4 jit_solution(16359119723385610459)
XLA Ops:
  0.7 0.8 %copy.168 = bf16[1,4,512]{2,0,1:T(2,128)(2,1)S(1)} copy(bf16[1,4,512]{2,1,0:T(4,128)(2,1)} %param.32) | data formatting | bytes 8192 | tf_op args[14]
  3.2 6.3 %all-to-all-start = ((bf16[4,2,256]{2,1,0:T(2,128)(2,1)}), bf16[4,2,256]{2,1,0:T(2,128)(2,1)}, u32[]{:S(2)}, u32[]{:S(2)}) async-start(bf16[4,2,256]{2,1,0:T(2,128)(2,1)} %reshape.510), calls=%async_computation | async-start | bytes 8192 | tf_op jit(solution)/shard_map/all_to_all | solution.py:128
  10.2 0.8 %negate_multiply_fusion = f32[1,128,32]{1,2,0:T(8,128)S(1)} fusion(f32[32]{0:T(128)} %param.25, f32[128]{0:T(128)S(1)} %compare_convert_fusion, f32[1,128,32]{1,2,0:T(8,128)} %param.22, f32[32]{0:T(128)} %param.26), kind=kLoop, calls=%fused_computation.73 | loop fusion | flops 40960 | bytes 33536 | tf_op jit(solution)/shard_map/while/body/eval_jaxpr/mul | solution.py:39
  13.2 0.9 %reshape.439 = bf16[128,4,128]{2,1,0:T(4,128)(2,1)S(1)} reshape(bf16[1,128,512]{2,1,0:T(8,128)(2,1)} %param.21) | data formatting | bytes 262144 | tf_op jit(solution)/shard_map/reshape.21
  14.1 1.0 %copy.129 = bf16[1,128,512]{1,2,0:T(8,128)(2,1)S(1)} copy(bf16[1,128,512]{2,1,0:T(8,128)(2,1)} %param.21) | data formatting | bytes 262144 | tf_op args[3]
  15.2 2.0 %copy.127 = bf16[1,128,2048]{1,2,0:T(8,128)(2,1)} copy(bf16[1,128,2048]{2,1,0:T(8,128)(2,1)} %param.18) | data formatting | bytes 1048576 | tf_op args[0]
  17.2 1.2 %copy.133 = f32[1,128,2048]{1,2,0:T(8,128)} copy(bf16[1,128,2048]{2,1,0:T(8,128)(2,1)S(1)} %copy-done.2) | data formatting | bytes 1572864 | tf_op jit(solution)/shard_map/while/body/eval_jaxpr/convert_element_type | solution.py:37
  18.4 0.8 %copy.136 = bf16[1,128,512]{1,2,0:T(8,128)(2,1)} copy(bf16[1,128,512]{2,1,0:T(8,128)(2,1)S(1)} %copy-done.6) | data formatting | bytes 262144 | tf_op args[2]
  20.3 0.7 %copy.125 = f32[128,32]{0,1:T(8,128)} copy(f32[128,32]{1,0:T(8,128)S(1)} %bitcast.135) | data formatting | bytes 32768 | tf_op jit(solution)/shard_map/while/body/eval_jaxpr/sub | solution.py:41
  22.8 0.7 %multiply_bitcast_fusion = (f32[128,32]{0,1:T(8,128)}, f32[128,32]{0,1:T(8,128)}) fusion(f32[1,128,32]{1,2,0:T(8,128)S(1)} %copy.138, f32[32]{0:T(128)S(1)} %slice_bitcast_fusion, f32[128]{0:T(128)S(1)} %compare_convert_fusion, f32[1,128,32]{1,2,0:T(8,128)S(1)} %copy-done.8, f32[32]{0:T(128)S(1)} %copy-done.18), kind=kLoop, calls=%fused_computation.72 | loop fusion | flops 40960 | bytes 66304 | tf_op jit(solution)/shard_map/while/body/eval_jaxpr/mul | solution.py:47
  23.7 0.8 %gather_fusion = f32[32,128,128]{1,2,0:T(8,128)S(1)} fusion(f32[128,128,4]{0,1,2:T(8,128)S(1)} %convolution_bitcast_fusion.1, s32[1024]{0:T(1024)} %pad_clamp_fusion.1), kind=kCustom, calls=%fused_computation.2 | custom fusion | bytes 4194432 | tf_op jit(solution)/shard_map/while/body/eval_jaxpr/jit(_take)/gather | solution.py:34
  24.5 1.9 %gather_fusion.2 = bf16[32,128,128]{2,1,0:T(8,128)(2,1)} fusion(bf16[128,4,128]{2,0,1:T(8,128)(2,1)S(1)} %bitcast.129, s32[1024]{0:T(1024)} %pad_clamp_fusion), kind=kCustom, calls=%fused_computation.clone | custom fusion | bytes 2097280 | tf_op jit(solution)/shard_map/while/body/eval_jaxpr/jit(_take)/gather | solution.py:36
  26.5 4.0 %fusion.12 = f32[1,128,32,64]{1,3,2,0:T(8,128)S(1)} fusion(bf16[128,32,64]{0,2,1:T(8,128)(2,1)} %bitcast.137, f32[32,128,128]{1,2,0:T(8,128)S(1)} %gather_fusion, f32[128,32]{0,1:T(8,128)S(1)} %copy-done.17, f32[128,32]{0,1:T(8,128)S(1)} %copy-done.12, pred[32]{0:T(512)(128)(4,1)S(1)} %copy-done.26, pred[128,128]{0,1:T(8,128)(4,1)S(1)} %copy-done.14), kind=kOutput, calls=%fused_computation.16 | convolution fusion | flops 405798912 | bytes 3719200 | tf_op jit(solution)/shard_map/while/body/eval_jaxpr/cijh,cjhp->cihp/dot_general | solution.py:44
  30.5 2.2 %fusion.17 = f32[1,128,32,64]{1,3,2,0:T(8,128)S(1)} fusion(f32[1,128,32,64]{1,3,2,0:T(8,128)S(1)} %fusion.12, f32[128,32,64]{0,2,1:T(8,128)S(1)} %bitcast.131, bf16[32,128,128]{2,1,0:T(8,128)(2,1)S(1)} %copy-done, f32[1,128,32,64]{1,3,2,0:T(8,128)S(1)} %bitcast.132, pred[32]{0:T(512)(128)(4,1)S(1)} %copy-done.26, f32[32]{0:T(128)S(1)} %copy-done.25, ...), kind=kOutput, calls=%fused_computation.20 | convolution fusion | flops 404226048 | bytes 5259424 | tf_op jit(solution)/shard_map/while/body/eval_jaxpr/cihn,cnhp->cihp/dot_general | solution.py:61
  33.8 1.8 %gather_fusion.3 = bf16[32,128,128]{2,1,0:T(8,128)(2,1)} fusion(bf16[128,4,128]{2,0,1:T(8,128)(2,1)S(1)} %bitcast.130, s32[1024]{0:T(1024)} %pad_clamp_fusion), kind=kCustom, calls=%fused_computation.1.clone | custom fusion | bytes 2097280 | tf_op jit(solution)/shard_map/while/body/eval_jaxpr/jit(_take)/gather | solution.py:35
  36.2 2.7 %fusion = f32[32,128,64]{1,2,0:T(8,128)S(1)} fusion(bf16[128,32,64]{0,2,1:T(8,128)(2,1)S(1)} %bitcast.138, bf16[32,128,128]{2,1,0:T(8,128)(2,1)} %gather_fusion.3, f32[128,32]{0,1:T(8,128)S(1)} %copy-done.16, pred[32]{0:T(512)(128)(4,1)S(1)} %copy-done.27), kind=kOutput, calls=%fused_computation.4 | convolution fusion | flops 404226048 | bytes 2637856 | tf_op jit(solution)/shard_map/while/body/eval_jaxpr/cjhn,cjhp->cnhp/dot_general | solution.py:46
  39.5 0.7 %reshape.511 = bf16[4,1,512]{2,1,0:T(2,128)(2,1)S(1)} reshape(bf16[4,2,256]{2,1,0:T(2,128)(2,1)} %all-to-all-done) | data formatting | bytes 8192
  40.2 0.7 %gather_fusion.1 = bf16[32,4,128]{2,1,0:T(4,128)(2,1)S(1)} fusion(bf16[4,4,128]{2,0,1:T(4,128)(2,1)S(1)} %bitcast.141, s32[1024]{0:T(1024)} %pad_clamp_fusion.1), kind=kCustom, calls=%fused_computation.3 | custom fusion | bytes 65664 | tf_op jit(solution)/shard_map/jit(_take)/gather | solution.py:80
  41.5 0.7 %reduce.7 = bf16[4,2048]{1,0:T(4,128)(2,1)S(1)} reduce(bf16[4,1,2048]{2,1,0:T(2,128)(2,1)S(1)} %convert_element_type.108, bf16[]{:T(256)} %broadcast.360), dimensions={1}, to_apply=%convert_element_type.108.reduce_sub_computation | reduce | bytes 32770 | tf_op jit(solution)/shard_map/convert_element_type | solution.py:133
  42.8 5.1 %all-to-all-start.1 = ((bf16[4,2,1024]{2,1,0:T(2,128)(2,1)}), bf16[4,2,1024]{2,1,0:T(2,128)(2,1)S(1)}, u32[]{:S(2)}, u32[]{:S(2)}) async-start(bf16[4,2,1024]{2,1,0:T(2,128)(2,1)} %reshape.512), calls=%async_computation.1 | async-start | bytes 32768 | tf_op jit(solution)/shard_map/all_to_all | solution.py:132
  48.1 1.0 %copy.145 = bf16[1,128,2048]{2,1,0:T(8,128)(2,1)} copy(bf16[1,128,2048]{1,2,0:T(8,128)(2,1)S(1)} %fusion.26) | data formatting | bytes 1048576
  49.5 4.0 %all-to-all-done.1 = bf16[4,2,1024]{2,1,0:T(2,128)(2,1)S(1)} async-done(((bf16[4,2,1024]{2,1,0:T(2,128)(2,1)}), bf16[4,2,1024]{2,1,0:T(2,128)(2,1)S(1)}, u32[]{:S(2)}, u32[]{:S(2)}) %all-to-all-start.1) | async-done | bytes 16416 | tf_op jit(solution)/shard_map/all_to_all | solution.py:132
  53.8 5.6 %all-reduce = (f32[1,128]{1,0:T(1,128)S(1)}, f32[1,4]{1,0:T(1,128)S(1)}) all-reduce(f32[1,128]{1,0:T(1,128)S(1)} %bitcast.143, f32[1,4]{1,0:T(1,128)S(1)} %bitcast.144), channel_id=1, replica_groups=mesh['rep'=2,'sample'=4,'head'=4] {'head'}, use_global_device_ids=true, to_apply=%region_2.4 | all-reduce | flops 132 | bytes 1056 | tf_op jit(solution)/shard_map/psum | solution.py:120
  60.2 1.2 %multiply_convert_fusion = bf16[1,128,2048]{2,1,0:T(8,128)(2,1)} fusion(f32[128]{0:T(128)S(1)} %copy-done.21, f32[2048]{0:T(1024)S(1)} %copy-done.9, f32[128]{0:T(128)S(1)} %rsqrt_bitcast_fusion.1, f32[1,128,2048]{2,1,0:T(8,128)S(1)} %copy.134, bf16[1,128,2048]{2,1,0:T(8,128)(2,1)S(1)} %copy-done.3), kind=kLoop, calls=%fused_computation.41 | loop fusion | flops 2621440 | bytes 2106368 | tf_op jit(solution)/shard_map/convert_element_type | solution.py:122
  (108 shorter events, 11.8 us)
Async XLA Ops:
  0.6 16.6 %copy-start.2 = (bf16[1,128,2048]{2,1,0:T(8,128)(2,1)S(1)}, bf16[1,128,2048]{2,1,0:T(8,128)(2,1)}, u32[]{:S(2)}) copy-start(bf16[1,128,2048]{2,1,0:T(8,128)(2,1)} %param.18) | copy-start | bytes 1572868
  0.6 17.8 %copy-start.6 = (bf16[1,128,512]{2,1,0:T(8,128)(2,1)S(1)}, bf16[1,128,512]{2,1,0:T(8,128)(2,1)}, u32[]{:S(2)}) copy-start(bf16[1,128,512]{2,1,0:T(8,128)(2,1)} %param.20) | copy-start | bytes 393220
  1.9 17.8 %copy-start.13 = (bf16[1,4,512]{2,1,0:T(4,128)(2,1)S(1)}, bf16[1,4,512]{2,1,0:T(4,128)(2,1)}, u32[]{:S(2)}) copy-start(bf16[1,4,512]{2,1,0:T(4,128)(2,1)} %param.32) | copy-start | bytes 12292
  3.2 36.3 %all-to-all-start = ((bf16[4,2,256]{2,1,0:T(2,128)(2,1)}), bf16[4,2,256]{2,1,0:T(2,128)(2,1)}, u32[]{:S(2)}, u32[]{:S(2)}) async-start(bf16[4,2,256]{2,1,0:T(2,128)(2,1)} %reshape.510), calls=%async_computation | async-start | bytes 8192 | tf_op jit(solution)/shard_map/all_to_all | solution.py:128
  10.2 12.5 %copy-start.20 = (f32[128]{0:T(128)}, f32[128]{0:T(128)S(1)}, u32[]{:S(2)}) copy-start(f32[128]{0:T(128)S(1)} %compare_convert_fusion) | copy-start | bytes 1540
  12.6 9.8 %copy-start.4 = (f32[1,128,2048]{2,1,0:T(8,128)S(1)}, f32[1,128,2048]{2,1,0:T(8,128)}, u32[]{:S(2)}) copy-start(f32[1,128,2048]{2,1,0:T(8,128)} %param.24) | copy-start | bytes 3145732
  17.2 5.6 %copy-start.8 = (f32[1,128,32]{1,2,0:T(8,128)S(1)}, f32[1,128,32]{1,2,0:T(8,128)}, u32[]{:S(2)}) copy-start(f32[1,128,32]{1,2,0:T(8,128)} %param.22) | copy-start | bytes 49156
  17.2 5.6 %copy-start.18 = (f32[32]{0:T(128)S(1)}, f32[32]{0:T(128)}, u32[]{:S(2)}) copy-start(f32[32]{0:T(128)} %param.26) | copy-start | bytes 388
  26.5 4.0 %copy-start = (bf16[32,128,128]{2,1,0:T(8,128)(2,1)S(1)}, bf16[32,128,128]{2,1,0:T(8,128)(2,1)}, u32[]{:S(2)}) copy-start(bf16[32,128,128]{2,1,0:T(8,128)(2,1)} %gather_fusion.2) | copy-start | bytes 3145732
  26.5 4.0 %copy-start.1 = (f32[1,128,2048]{1,2,0:T(8,128)S(1)}, f32[1,128,2048]{1,2,0:T(8,128)}, u32[]{:S(2)}) copy-start(f32[1,128,2048]{1,2,0:T(8,128)} %copy.133) | copy-start | bytes 3145732
  26.5 4.0 %copy-start.25 = (f32[32]{0:T(128)S(1)}, f32[32]{0:T(128)}, u32[]{:S(2)}) copy-start(f32[32]{0:T(128)} %param.27) | copy-start | bytes 388
  32.8 3.0 %copy-start.22 = (bf16[1,4,512]{2,1,0:T(4,128)(2,1)S(1)}, bf16[1,4,512]{2,1,0:T(4,128)(2,1)}, u32[]{:S(2)}) copy-start(bf16[1,4,512]{2,1,0:T(4,128)(2,1)} %param.31) | copy-start | bytes 12292
  32.8 3.0 %copy-start.19 = (f32[32]{0:T(128)S(1)}, f32[32]{0:T(128)}, u32[]{:S(2)}) copy-start(f32[32]{0:T(128)} %param.26) | copy-start | bytes 388
  32.8 3.0 %copy-start.23 = (f32[32]{0:T(128)S(1)}, f32[32]{0:T(128)}, u32[]{:S(2)}) copy-start(f32[32]{0:T(128)} %param.25) | copy-start | bytes 388
  33.2 3.0 %copy-start.5 = (bf16[1,128,2048]{1,2,0:T(8,128)(2,1)S(1)}, bf16[1,128,2048]{1,2,0:T(8,128)(2,1)}, u32[]{:S(2)}) copy-start(bf16[1,128,2048]{1,2,0:T(8,128)(2,1)} %copy.127) | copy-start | bytes 1572868
  33.2 3.0 %copy-start.16 = (f32[128,32]{0,1:T(8,128)S(1)}, f32[128,32]{0,1:T(8,128)}, u32[]{:S(2)}) copy-start(f32[128,32]{0,1:T(8,128)} %get-tuple-element.76) | copy-start | bytes 49156
  33.2 3.0 %copy-start.27 = (pred[32]{0:T(512)(128)(4,1)S(1)}, pred[32]{0:T(512)(128)(4,1)}, u32[]{:S(2)}) copy-start(pred[32]{0:T(512)(128)(4,1)} %compare_and_fusion) | copy-start | bytes 100
  36.2 3.2 %copy-start.15 = (bf16[4,4,128]{2,1,0:T(4,128)(2,1)S(1)}, bf16[4,4,128]{2,1,0:T(4,128)(2,1)}, u32[]{:S(2)}) copy-start(bf16[4,4,128]{2,1,0:T(4,128)(2,1)} %reshape.449) | copy-start | bytes 12292
  39.0 9.0 %copy-start.29 = (s32[32]{0:T(128)S(1)}, s32[32]{0:T(128)}, u32[]{:S(2)}) copy-start(s32[32]{0:T(128)} %get-tuple-element.79) | copy-start | bytes 388
  39.0 14.6 %copy-start.10 = (bf16[1,4,2048]{2,1,0:T(4,128)(2,1)S(1)}, bf16[1,4,2048]{2,1,0:T(4,128)(2,1)}, u32[]{:S(2)}) copy-start(bf16[1,4,2048]{2,1,0:T(4,128)(2,1)} %param.30) | copy-start | bytes 49156
  39.0 14.6 %copy-start.11 = (bf16[1,4,2048]{2,1,0:T(4,128)(2,1)S(1)}, bf16[1,4,2048]{2,1,0:T(4,128)(2,1)}, u32[]{:S(2)}) copy-start(bf16[1,4,2048]{2,1,0:T(4,128)(2,1)} %param.29) | copy-start | bytes 49156
  39.0 20.5 %copy-start.9 = (f32[2048]{0:T(1024)S(1)}, f32[2048]{0:T(1024)}, u32[]{:S(2)}) copy-start(f32[2048]{0:T(1024)} %param.28) | copy-start | bytes 24580
  39.0 21.2 %copy-start.21 = (f32[128]{0:T(128)S(1)}, f32[128]{0:T(128)}, u32[]{:S(2)}) copy-start(f32[128]{0:T(128)} %copy-done.20) | copy-start | bytes 1540
  42.8 10.7 %all-to-all-start.1 = ((bf16[4,2,1024]{2,1,0:T(2,128)(2,1)}), bf16[4,2,1024]{2,1,0:T(2,128)(2,1)S(1)}, u32[]{:S(2)}, u32[]{:S(2)}) async-start(bf16[4,2,1024]{2,1,0:T(2,128)(2,1)} %reshape.512), calls=%async_computation.1 | async-start | bytes 32768 | tf_op jit(solution)/shard_map/all_to_all | solution.py:132
  (8 other events, 17.2 us)
where the time goes:
time: 62.1 us; the launch traced here: 61.4 us
  local copies, waits for them, and re-layouts  20.3 us (33%)
  starting transfers between devices  11.4 us (18%)
  matrix products  9.71 us (16%)
  other arithmetic  8.5 us (14%)
  blocking collectives  5.63 us (9%)
  waiting for transfers between devices  4.02 us (6%)
  between operations  1.81 us (3%)
    unnamed x72, local copies, waits for them, and re-layouts  9.6 us
    all_to_all x1, starting transfers between devices, body(): lax.all_to_all(c_dec, 'sample', split_axis=1, concat_axis=0, tiled=True)  6.35 us
    psum x1, blocking collectives, body(): pre_totals = lax.psum(jnp.sum(gated_rows * gated_rows, axis=-1), 'head')  5.63 us
    all_to_all x1, starting transfers between devices, body(): lax.all_to_all(answers.astype(jnp.bfloat16), 'sample', split_axis=0, conc...  5.09 us
    all_to_all x1, waiting for transfers between devices, body(): lax.all_to_all(answers.astype(jnp.bfloat16), 'sample', split_axis=0, conc...  4.01 us
    dot_general x1, matrix products, scan_prompt(): jnp.einsum('cijh,cjhp->cihp', scores, values, precision=highest)  3.96 us
    dot_general x1, matrix products, scan_prompt(): jnp.einsum('cjhn,cjhp->cnhp', b_head * tail_decay[..., None], values, pre...  2.73 us
    dot_general x1, matrix products, scan_prompt(): jnp.einsum('cihn,cnhp->cihp', c_head, starts, precision=highest)  2.2 us
  transfers between devices with their start and end apart: 2, of which 1 were waited for; matrix products, arithmetic and copies ran while one was open for 49% of the time, Pallas kernels for 0%

commit v1 on v0

--- a/solution.py
+++ b/solution.py
@@ -117,7 +117,9 @@
     result, final_carry = lax.map(one_prompt, (x_pre, b_pre, c_pre, step_delta, init_state))
     final_state = final_carry.astype(jnp.bfloat16)
     gated_rows = gate_values(result, z_pre)
-    pre_totals = lax.psum(jnp.sum(gated_rows * gated_rows, axis=-1), "head")
+    block = jnp.sum(gated_rows * gated_rows, axis=-1)
+    parts = lax.all_gather(block, "head")
+    pre_totals = jnp.sum(parts, axis=0)
     norm_scale = lax.rsqrt(pre_totals[:, :, None] / (H * P_SIZE) + epsilon)
     out_pre = (gated_rows * norm_scale * norm_gain * valid_mask[:, :, None]).astype(jnp.bfloat16)
     slots_here = x_dec.shape[0]

time: 62.1 us -> 66.8 us (1.076)
  blocking collectives: 5.63 us -> 10.7 us
  matrix products: 9.71 us -> 8.66 us
  other arithmetic: 8.5 us -> 9.48 us
    all_gather x0 -> x1, blocking collectives: none -> 5.06 us  [body(): parts = lax.all_gather(block, 'head')]
    reduce_sum x1 -> x2, other arithmetic: 0.41 us -> 1.51 us  [the longest x1 1.49 us: body(): block = jnp.sum(gated_rows * gated_rows, axis=-1)]
    dot_general x1, matrix products: 2.73 us -> 1.68 us  [scan_prompt(): jnp.einsum('cjhn,cjhp->cnhp', b_head * tail_decay[..., None], values, pre...]
  transfers between devices with their start and end apart: 2 -> 2, of which waited for: 1 -> 1; matrix products, arithmetic and copies ran while one was open for 49% -> 47% of each run, Pallas kernels for 0% -> 0%
where the time goes in v1:
time: 66.8 us; the launch traced here: 66.1 us
  local copies, waits for them, and re-layouts  20 us (30%)
  starting transfers between devices  11.4 us (17%)
  blocking collectives  10.7 us (16%)
  other arithmetic  9.48 us (14%)
  matrix products  8.66 us (13%)
  waiting for transfers between devices  4.02 us (6%)
  between operations  1.8 us (3%)
    unnamed x72, local copies, waits for them, and re-layouts  9.16 us
    all_to_all x1, starting transfers between devices, body(): lax.all_to_all(c_dec, 'sample', split_axis=1, concat_axis=0, tiled=True)  6.35 us
    psum x1, blocking collectives, body(): dec_totals = lax.psum(jnp.sum(gated_dec * gated_dec, axis=-1), 'head')  5.63 us
    all_to_all x1, starting transfers between devices, body(): lax.all_to_all(answers.astype(jnp.bfloat16), 'sample', split_axis=0, conc...  5.09 us
    all_gather x1, blocking collectives, body(): parts = lax.all_gather(block, 'head')  5.06 us
    all_to_all x1, waiting for transfers between devices, body(): lax.all_to_all(answers.astype(jnp.bfloat16), 'sample', split_axis=0, conc...  4.01 us
    dot_general x1, matrix products, scan_prompt(): jnp.einsum('cijh,cjhp->cihp', scores, values, precision=highest)  3.96 us
    dot_general x1, matrix products, scan_prompt(): jnp.einsum('cihn,cnhp->cihp', c_head, starts, precision=highest)  2.2 us
  transfers between devices with their start and end apart: 2, of which 1 were waited for; matrix products, arithmetic and copies ran while one was open for 47% of the time, Pallas kernels for 0%

profile of v1, /device:TPU:0, one launch (start us, length us, event | category | flops | bytes accessed | tf_op | source)
XLA Modules:
  0.0 66.1 jit_solution(13002857377517609837)
XLA Ops:
  0.7 0.8 %copy.168 = bf16[1,4,512]{2,0,1:T(2,128)(2,1)S(1)} copy(bf16[1,4,512]{2,1,0:T(4,128)(2,1)} %param.32) | data formatting | bytes 8192 | tf_op args[14]
  3.1 6.3 %all-to-all-start = ((bf16[4,2,256]{2,1,0:T(2,128)(2,1)}), bf16[4,2,256]{2,1,0:T(2,128)(2,1)}, u32[]{:S(2)}, u32[]{:S(2)}) async-start(bf16[4,2,256]{2,1,0:T(2,128)(2,1)} %reshape.511), calls=%async_computation | async-start | bytes 8192 | tf_op jit(solution)/shard_map/all_to_all | solution.py:130
  10.1 0.8 %negate_multiply_fusion = f32[1,128,32]{1,2,0:T(8,128)S(1)} fusion(f32[32]{0:T(128)} %param.25, f32[128]{0:T(128)S(1)} %compare_convert_fusion, f32[1,128,32]{1,2,0:T(8,128)} %param.22, f32[32]{0:T(128)} %param.26), kind=kLoop, calls=%fused_computation.73 | loop fusion | flops 40960 | bytes 33536 | tf_op jit(solution)/shard_map/while/body/eval_jaxpr/mul | solution.py:39
  13.1 0.9 %reshape.435 = bf16[128,4,128]{2,1,0:T(4,128)(2,1)S(1)} reshape(bf16[1,128,512]{2,1,0:T(8,128)(2,1)} %param.21) | data formatting | bytes 262144 | tf_op jit(solution)/shard_map/reshape.21
  14.0 1.0 %copy.129 = bf16[1,128,512]{1,2,0:T(8,128)(2,1)S(1)} copy(bf16[1,128,512]{2,1,0:T(8,128)(2,1)} %param.21) | data formatting | bytes 262144 | tf_op args[3]
  15.1 2.0 %copy.127 = bf16[1,128,2048]{1,2,0:T(8,128)(2,1)} copy(bf16[1,128,2048]{2,1,0:T(8,128)(2,1)} %param.18) | data formatting | bytes 1048576 | tf_op args[0]
  17.1 1.2 %copy.133 = f32[1,128,2048]{1,2,0:T(8,128)} copy(bf16[1,128,2048]{2,1,0:T(8,128)(2,1)S(1)} %copy-done.2) | data formatting | bytes 1572864 | tf_op jit(solution)/shard_map/while/body/eval_jaxpr/convert_element_type | solution.py:37
  18.3 0.8 %copy.136 = bf16[1,128,512]{1,2,0:T(8,128)(2,1)} copy(bf16[1,128,512]{2,1,0:T(8,128)(2,1)S(1)} %copy-done.7) | data formatting | bytes 262144 | tf_op args[2]
  22.7 0.7 %multiply_bitcast_fusion = (f32[128,32]{0,1:T(8,128)}, f32[128,32]{0,1:T(8,128)}) fusion(f32[1,128,32]{1,2,0:T(8,128)S(1)} %copy.138, f32[32]{0:T(128)S(1)} %slice_bitcast_fusion, f32[128]{0:T(128)S(1)} %compare_convert_fusion, f32[1,128,32]{1,2,0:T(8,128)S(1)} %copy-done.9, f32[32]{0:T(128)S(1)} %copy-done.19), kind=kLoop, calls=%fused_computation.72 | loop fusion | flops 40960 | bytes 66304 | tf_op jit(solution)/shard_map/while/body/eval_jaxpr/mul | solution.py:47
  23.7 0.8 %gather_fusion = f32[32,128,128]{1,2,0:T(8,128)S(1)} fusion(f32[128,128,4]{0,1,2:T(8,128)S(1)} %convolution_bitcast_fusion.1, s32[1024]{0:T(1024)} %pad_clamp_fusion.1), kind=kCustom, calls=%fused_computation.2 | custom fusion | bytes 4194432 | tf_op jit(solution)/shard_map/while/body/eval_jaxpr/jit(_take)/gather | solution.py:34
  24.5 2.0 %gather_fusion.2 = bf16[32,128,128]{2,1,0:T(8,128)(2,1)} fusion(bf16[128,4,128]{2,0,1:T(8,128)(2,1)S(1)} %bitcast.127, s32[1024]{0:T(1024)} %pad_clamp_fusion), kind=kCustom, calls=%fused_computation.clone | custom fusion | bytes 2097280 | tf_op jit(solution)/shard_map/while/body/eval_jaxpr/jit(_take)/gather | solution.py:36
  26.5 4.0 %fusion.12 = f32[1,128,32,64]{1,3,2,0:T(8,128)S(1)} fusion(bf16[128,32,64]{0,2,1:T(8,128)(2,1)} %bitcast.135, f32[32,128,128]{1,2,0:T(8,128)S(1)} %gather_fusion, f32[128,32]{0,1:T(8,128)S(1)} %copy-done.18, f32[128,32]{0,1:T(8,128)S(1)} %copy-done.13, pred[32]{0:T(512)(128)(4,1)S(1)} %copy-done.27, pred[128,128]{0,1:T(8,128)(4,1)S(1)} %copy-done.15), kind=kOutput, calls=%fused_computation.16 | convolution fusion | flops 405798912 | bytes 3719200 | tf_op jit(solution)/shard_map/while/body/eval_jaxpr/cijh,cjhp->cihp/dot_general | solution.py:44
  30.5 2.2 %fusion.17 = f32[1,128,32,64]{1,3,2,0:T(8,128)S(1)} fusion(f32[1,128,32,64]{1,3,2,0:T(8,128)S(1)} %fusion.12, f32[128,32,64]{0,2,1:T(8,128)S(1)} %bitcast.129, bf16[32,128,128]{2,1,0:T(8,128)(2,1)S(1)} %copy-done, f32[1,128,32,64]{1,3,2,0:T(8,128)S(1)} %bitcast.130, pred[32]{0:T(512)(128)(4,1)S(1)} %copy-done.27, f32[32]{0:T(128)S(1)} %copy-done.26, ...), kind=kOutput, calls=%fused_computation.20 | convolution fusion | flops 404226048 | bytes 5259424 | tf_op jit(solution)/shard_map/while/body/eval_jaxpr/cihn,cnhp->cihp/dot_general | solution.py:61
  33.2 1.5 %multiply_reduce_fusion = f32[128]{0:T(128)S(1)} fusion(f32[1,128,2048]{2,1,0:T(8,128)S(1)} %copy.134, bf16[1,128,2048]{2,1,0:T(8,128)(2,1)} %param.19), kind=kLoop, calls=%fused_computation.42 | loop fusion | flops 2097024 | bytes 1573376 | tf_op jit(solution)/shard_map/reduce_sum | solution.py:120
  34.7 5.1 %all-gather.1 = f32[4,1,128]{2,1,0:T(1,128)S(1)} all-gather(f32[1,1,128]{2,1,0:T(1,128)S(1)} %bitcast.141), channel_id=2, replica_groups=mesh['rep'=2,'sample'=4,'head'=4] {'head'}, dimensions={0}, use_global_device_ids=true | all-gather | bytes 2560 | tf_op jit(solution)/shard_map/all_gather | solution.py:121
  39.9 1.9 %gather_fusion.3 = bf16[32,128,128]{2,1,0:T(8,128)(2,1)} fusion(bf16[128,4,128]{2,0,1:T(8,128)(2,1)S(1)} %bitcast.128, s32[1024]{0:T(1024)} %pad_clamp_fusion), kind=kCustom, calls=%fused_computation.1.clone | custom fusion | bytes 2097280 | tf_op jit(solution)/shard_map/while/body/eval_jaxpr/jit(_take)/gather | solution.py:35
  42.1 1.2 %multiply_convert_fusion = bf16[1,128,2048]{2,1,0:T(8,128)(2,1)} fusion(f32[128]{0:T(128)S(1)} %copy-done.22, f32[2048]{0:T(1024)S(1)} %copy-done.10, f32[128]{0:T(128)S(1)} %add_rsqrt_fusion, f32[1,128,2048]{2,1,0:T(8,128)S(1)} %copy.134, bf16[1,128,2048]{2,1,0:T(8,128)(2,1)S(1)} %copy-done.3), kind=kLoop, calls=%fused_computation.41 | loop fusion | flops 2621440 | bytes 2106368 | tf_op jit(solution)/shard_map/convert_element_type | solution.py:124
  43.3 1.7 %fusion = f32[32,128,64]{1,2,0:T(8,128)S(1)} fusion(bf16[128,32,64]{0,2,1:T(8,128)(2,1)S(1)} %bitcast.136, bf16[32,128,128]{2,1,0:T(8,128)(2,1)S(1)} %copy-done.4, f32[128,32]{0,1:T(8,128)S(1)} %copy-done.17, pred[32]{0:T(512)(128)(4,1)S(1)} %copy-done.27), kind=kOutput, calls=%fused_computation.4 | convolution fusion | flops 404226048 | bytes 2637856 | tf_op jit(solution)/shard_map/while/body/eval_jaxpr/cjhn,cjhp->cnhp/dot_general | solution.py:46
  45.5 0.7 %reshape.512 = bf16[4,1,512]{2,1,0:T(2,128)(2,1)S(1)} reshape(bf16[4,2,256]{2,1,0:T(2,128)(2,1)} %all-to-all-done) | data formatting | bytes 8192
  46.2 0.7 %gather_fusion.1 = bf16[32,4,128]{2,1,0:T(4,128)(2,1)S(1)} fusion(bf16[4,4,128]{2,0,1:T(4,128)(2,1)S(1)} %bitcast.139, s32[1024]{0:T(1024)} %pad_clamp_fusion.1), kind=kCustom, calls=%fused_computation.3 | custom fusion | bytes 65664 | tf_op jit(solution)/shard_map/jit(_take)/gather | solution.py:80
  48.8 5.1 %all-to-all-start.1 = ((bf16[4,2,1024]{2,1,0:T(2,128)(2,1)}), bf16[4,2,1024]{2,1,0:T(2,128)(2,1)S(1)}, u32[]{:S(2)}, u32[]{:S(2)}) async-start(bf16[4,2,1024]{2,1,0:T(2,128)(2,1)} %reshape.513), calls=%async_computation.1 | async-start | bytes 32768 | tf_op jit(solution)/shard_map/all_to_all | solution.py:134
  54.0 1.0 %copy.145 = bf16[1,128,2048]{2,1,0:T(8,128)(2,1)} copy(bf16[1,128,2048]{1,2,0:T(8,128)(2,1)S(1)} %fusion.26) | data formatting | bytes 1048576
  55.4 4.0 %all-to-all-done.1 = bf16[4,2,1024]{2,1,0:T(2,128)(2,1)S(1)} async-done(((bf16[4,2,1024]{2,1,0:T(2,128)(2,1)}), bf16[4,2,1024]{2,1,0:T(2,128)(2,1)S(1)}, u32[]{:S(2)}, u32[]{:S(2)}) %all-to-all-start.1) | async-done | bytes 16416 | tf_op jit(solution)/shard_map/all_to_all | solution.py:134
  59.7 5.6 %psum.7 = f32[1,4]{1,0:T(1,128)S(1)} all-reduce(f32[1,4]{1,0:T(1,128)S(1)} %bitcast.142), channel_id=1, replica_groups=mesh['rep'=2,'sample'=4,'head'=4] {'head'}, use_global_device_ids=true, to_apply=%region_4.6 | all-reduce | flops 4 | bytes 32 | tf_op jit(solution)/shard_map/psum | solution.py:151
  (110 shorter events, 12.3 us)
Async XLA Ops:
  0.6 16.5 %copy-start.2 = (bf16[1,128,2048]{2,1,0:T(8,128)(2,1)S(1)}, bf16[1,128,2048]{2,1,0:T(8,128)(2,1)}, u32[]{:S(2)}) copy-start(bf16[1,128,2048]{2,1,0:T(8,128)(2,1)} %param.18) | copy-start | bytes 1572868
  0.6 17.7 %copy-start.7 = (bf16[1,128,512]{2,1,0:T(8,128)(2,1)S(1)}, bf16[1,128,512]{2,1,0:T(8,128)(2,1)}, u32[]{:S(2)}) copy-start(bf16[1,128,512]{2,1,0:T(8,128)(2,1)} %param.20) | copy-start | bytes 393220
  1.9 17.8 %copy-start.14 = (bf16[1,4,512]{2,1,0:T(4,128)(2,1)S(1)}, bf16[1,4,512]{2,1,0:T(4,128)(2,1)}, u32[]{:S(2)}) copy-start(bf16[1,4,512]{2,1,0:T(4,128)(2,1)} %param.32) | copy-start | bytes 12292
  3.1 42.3 %all-to-all-start = ((bf16[4,2,256]{2,1,0:T(2,128)(2,1)}), bf16[4,2,256]{2,1,0:T(2,128)(2,1)}, u32[]{:S(2)}, u32[]{:S(2)}) async-start(bf16[4,2,256]{2,1,0:T(2,128)(2,1)} %reshape.511), calls=%async_computation | async-start | bytes 8192 | tf_op jit(solution)/shard_map/all_to_all | solution.py:130
  10.1 12.6 %copy-start.21 = (f32[128]{0:T(128)}, f32[128]{0:T(128)S(1)}, u32[]{:S(2)}) copy-start(f32[128]{0:T(128)S(1)} %compare_convert_fusion) | copy-start | bytes 1540
  12.5 9.9 %copy-start.5 = (f32[1,128,2048]{2,1,0:T(8,128)S(1)}, f32[1,128,2048]{2,1,0:T(8,128)}, u32[]{:S(2)}) copy-start(f32[1,128,2048]{2,1,0:T(8,128)} %param.24) | copy-start | bytes 3145732
  17.1 5.6 %copy-start.9 = (f32[1,128,32]{1,2,0:T(8,128)S(1)}, f32[1,128,32]{1,2,0:T(8,128)}, u32[]{:S(2)}) copy-start(f32[1,128,32]{1,2,0:T(8,128)} %param.22) | copy-start | bytes 49156
  17.1 5.6 %copy-start.19 = (f32[32]{0:T(128)S(1)}, f32[32]{0:T(128)}, u32[]{:S(2)}) copy-start(f32[32]{0:T(128)} %param.26) | copy-start | bytes 388
  26.5 4.0 %copy-start = (bf16[32,128,128]{2,1,0:T(8,128)(2,1)S(1)}, bf16[32,128,128]{2,1,0:T(8,128)(2,1)}, u32[]{:S(2)}) copy-start(bf16[32,128,128]{2,1,0:T(8,128)(2,1)} %gather_fusion.2) | copy-start | bytes 3145732
  26.5 4.0 %copy-start.1 = (f32[1,128,2048]{1,2,0:T(8,128)S(1)}, f32[1,128,2048]{1,2,0:T(8,128)}, u32[]{:S(2)}) copy-start(f32[1,128,2048]{1,2,0:T(8,128)} %copy.133) | copy-start | bytes 3145732
  26.5 4.0 %copy-start.26 = (f32[32]{0:T(128)S(1)}, f32[32]{0:T(128)}, u32[]{:S(2)}) copy-start(f32[32]{0:T(128)} %param.27) | copy-start | bytes 388
  32.7 7.0 %copy-start.8 = (bf16[1,128,512]{1,2,0:T(8,128)(2,1)S(1)}, bf16[1,128,512]{1,2,0:T(8,128)(2,1)}, u32[]{:S(2)}) copy-start(bf16[1,128,512]{1,2,0:T(8,128)(2,1)} %copy.136) | copy-start | bytes 393220
  33.1 8.8 %copy-start.28 = (f32[32]{0:T(128)S(1)}, f32[32]{0:T(128)}, u32[]{:S(2)}) copy-start(f32[32]{0:T(128)} %fusion.59) | copy-start | bytes 388
  33.1 8.9 %copy-start.23 = (bf16[1,4,512]{2,1,0:T(4,128)(2,1)S(1)}, bf16[1,4,512]{2,1,0:T(4,128)(2,1)}, u32[]{:S(2)}) copy-start(bf16[1,4,512]{2,1,0:T(4,128)(2,1)} %param.31) | copy-start | bytes 12292
  33.1 8.9 %copy-start.20 = (f32[32]{0:T(128)S(1)}, f32[32]{0:T(128)}, u32[]{:S(2)}) copy-start(f32[32]{0:T(128)} %param.26) | copy-start | bytes 388
  33.1 8.9 %copy-start.24 = (f32[32]{0:T(128)S(1)}, f32[32]{0:T(128)}, u32[]{:S(2)}) copy-start(f32[32]{0:T(128)} %param.25) | copy-start | bytes 388
  33.1 8.9 %copy-start.25 = (f32[1,4,32]{2,1,0:T(4,128)S(1)}, f32[1,4,32]{2,1,0:T(4,128)}, u32[]{:S(2)}) copy-start(f32[1,4,32]{2,1,0:T(4,128)} %param.33) | copy-start | bytes 1540
  33.1 8.9 %copy-start.3 = (bf16[1,128,2048]{2,1,0:T(8,128)(2,1)S(1)}, bf16[1,128,2048]{2,1,0:T(8,128)(2,1)}, u32[]{:S(2)}) copy-start(bf16[1,128,2048]{2,1,0:T(8,128)(2,1)} %param.19) | copy-start | bytes 1572868
  33.1 8.9 %copy-start.10 = (f32[2048]{0:T(1024)S(1)}, f32[2048]{0:T(1024)}, u32[]{:S(2)}) copy-start(f32[2048]{0:T(1024)} %param.28) | copy-start | bytes 24580
  33.2 8.9 %copy-start.22 = (f32[128]{0:T(128)S(1)}, f32[128]{0:T(128)}, u32[]{:S(2)}) copy-start(f32[128]{0:T(128)} %copy-done.21) | copy-start | bytes 1540
  45.0 8.9 %copy-start.29 = (s32[32]{0:T(128)S(1)}, s32[32]{0:T(128)}, u32[]{:S(2)}) copy-start(s32[32]{0:T(128)} %get-tuple-element.77) | copy-start | bytes 388
  45.0 14.5 %copy-start.11 = (bf16[1,4,2048]{2,1,0:T(4,128)(2,1)S(1)}, bf16[1,4,2048]{2,1,0:T(4,128)(2,1)}, u32[]{:S(2)}) copy-start(bf16[1,4,2048]{2,1,0:T(4,128)(2,1)} %param.30) | copy-start | bytes 49156
  45.0 14.5 %copy-start.12 = (bf16[1,4,2048]{2,1,0:T(4,128)(2,1)S(1)}, bf16[1,4,2048]{2,1,0:T(4,128)(2,1)}, u32[]{:S(2)}) copy-start(bf16[1,4,2048]{2,1,0:T(4,128)(2,1)} %param.29) | copy-start | bytes 49156
  48.8 10.7 %all-to-all-start.1 = ((bf16[4,2,1024]{2,1,0:T(2,128)(2,1)}), bf16[4,2,1024]{2,1,0:T(2,128)(2,1)S(1)}, u32[]{:S(2)}, u32[]{:S(2)}) async-start(bf16[4,2,1024]{2,1,0:T(2,128)(2,1)} %reshape.513), calls=%async_computation.1 | async-start | bytes 32768 | tf_op jit(solution)/shard_map/all_to_all | solution.py:134
  (8 other events, 18.0 us)
